TPU v7x, 512 devices: a whole 4x8x8 slice. The times are simulated.
512 devices in a mesh: dp: 32 (over x, y_hi, core), fsdp: 16 (over y_lo, z).
Axes of the slice: x: 4, y: 8 (y_hi: 4, y_lo: 2; y = y_hi * 2 + y_lo), z: 8, core: 2. Of those that a mesh axis runs over, the one named last changes fastest.
Arguments:
- hidden: bfloat16 [4, 2048, 16, 4096], P(None, 'dp', 'fsdp'), may hold values from -6 to 6
- frozen_query_rows: bfloat16 [4, 2048, 16, 2048], P(None, 'dp', 'fsdp'), may hold values from -10 to 10
- output_gradient: bfloat16 [4, 2048, 16, 2048], P(None, 'dp', 'fsdp'), may hold values from -6 to 6
- token_log_ratio: float32 [4, 2048, 16], P(None, 'dp', 'fsdp'), may hold values from -0.15625 to 0.15625
- lengths: int32 [4], replicated, may hold values from 1 to 32768, as said below
- response_win_probability: float32 [4], replicated, may hold values from 0.05 to 0.95
- cached_prompt_keys: bfloat16 [1024, 512], P('fsdp'), may hold values from -7.5 to 7.5
- cached_prompt_values: bfloat16 [1024, 512], P('fsdp'), may hold values from -6 to 6
- adapter_down_factor: bfloat16 [4096, 64], P('fsdp'), may hold values from -0.09375 to 0.09375
- adapter_up_factor: bfloat16 [64, 2048], P(None, 'fsdp'), may hold values from -0.125 to 0.125
- attention_norm_gain: bfloat16 [4096], P('fsdp'), may hold values from 0.5 to 1.5
Outputs:
- grad_down: float32 [4096, 64], P('fsdp')
- grad_up: float32 [64, 2048], P(None, 'fsdp')
- seq_ratio: float32 [4], replicated
Inputs may be any that keep to these rules, and one draw needn't show every extreme that they name: The lengths sum to 65472 and the longest is exactly 32768.
All inputs are finite; a program needn't handle non-finite values.
Results may differ from a plain program's by a relative error of at most 0.012.
Values may be sent and summed in bfloat16 or wider, within the bound.
A program may use at most 128 MiB of HBM per device.

v0:
```python
import math
import jax
import jax.numpy as jnp
from jax import lax
from jax.sharding import PartitionSpec as P

HEAD_SIZE = 128
QUERY_HEADS = 16
KEY_VALUE_HEADS = 4
target_scale = 1.0
norm_epsilon = 1e-05


def attend(query_vectors, cotangent, key_rows, value_rows):
    row_count = query_vectors.shape[0]
    queries_per_group = QUERY_HEADS // KEY_VALUE_HEADS
    score_scale = 1.0 / math.sqrt(HEAD_SIZE)
    pieces = []
    for shared_key_head in range(KEY_VALUE_HEADS):
        head_start = shared_key_head * queries_per_group * HEAD_SIZE
        head_stop = head_start + queries_per_group * HEAD_SIZE
        head_query = query_vectors[:, head_start:head_stop].reshape(
            row_count, queries_per_group, HEAD_SIZE
        )
        head_grad = cotangent[:, head_start:head_stop].reshape(
            row_count, queries_per_group, HEAD_SIZE
        )
        head_key = key_rows[:, shared_key_head * HEAD_SIZE : (shared_key_head + 1) * HEAD_SIZE]
        head_value = value_rows[:, shared_key_head * HEAD_SIZE : (shared_key_head + 1) * HEAD_SIZE]
        scores = (
            jnp.einsum("nhd,jd->nhj", head_query, head_key, preferred_element_type=jnp.float32)
            * score_scale
        )
        row_top = jnp.max(scores, axis=2, keepdims=True)
        exponent = jnp.exp(scores - row_top)
        row_total = jnp.sum(exponent, axis=2, keepdims=True)
        weights = exponent.astype(jnp.bfloat16)
        mixed_out = (
            jnp.einsum("nhj,jd->nhd", weights, head_value, preferred_element_type=jnp.float32)
            / row_total
        )
        inner_prod = jnp.sum(head_grad.astype(jnp.float32) * mixed_out, axis=2, keepdims=True)
        grad_prob = jnp.einsum(
            "nhd,jd->nhj", head_grad, head_value, preferred_element_type=jnp.float32
        )
        grad_score = (weights.astype(jnp.float32) / row_total * (grad_prob - inner_prod)).astype(
            jnp.bfloat16
        )
        query_gradient = (
            jnp.einsum("nhj,jd->nhd", grad_score, head_key, preferred_element_type=jnp.float32)
            * score_scale
        )
        pieces.append(query_gradient.reshape(row_count, queries_per_group * HEAD_SIZE))
    return jnp.concatenate(pieces, axis=1).astype(jnp.bfloat16)


def body(
    hidden,
    frozen_query_rows,
    output_gradient,
    token_log_ratio,
    lengths,
    response_win_probability,
    cached_prompt_keys,
    cached_prompt_values,
    adapter_down_factor,
    adapter_up_factor,
    attention_norm_gain,
):
    fsdp_count = lax.axis_size("fsdp")
    dp_index = lax.axis_index("dp")
    fsdp_index = lax.axis_index("fsdp")
    responses, per_device, single, feature_count = hidden.shape
    home_rows = responses * per_device
    local_rows = jnp.arange(per_device, dtype=jnp.int32)
    position = (dp_index * per_device + local_rows) * fsdp_count + fsdp_index
    is_valid = position[None, :] < lengths[:, None]
    partial_value = jnp.sum(jnp.where(is_valid, token_log_ratio[:, :, 0], 0.0), axis=1)
    seq_ratio = lax.psum(partial_value, ("dp", "fsdp"))
    weighting = 2.0 * (seq_ratio - target_scale * (response_win_probability - 0.5)) / responses
    down_full, up_full, gain_full = (
        lax.all_gather(adapter_down_factor, "fsdp", axis=0, tiled=True),
        lax.all_gather(adapter_up_factor, "fsdp", axis=1, tiled=True),
        lax.all_gather(attention_norm_gain, "fsdp", axis=0, tiled=True),
    )
    key_rows, value_rows = (
        lax.all_gather(cached_prompt_keys, "fsdp", axis=0, tiled=True),
        lax.all_gather(cached_prompt_values, "fsdp", axis=0, tiled=True),
    )
    widened = hidden.reshape(home_rows, feature_count).astype(jnp.float32)
    inverse = lax.rsqrt(jnp.mean(widened * widened, axis=1, keepdims=True) + norm_epsilon)
    normed_input = (widened * inverse * gain_full.astype(jnp.float32)).astype(jnp.bfloat16)
    lowrank_hidden = jnp.dot(normed_input, down_full, preferred_element_type=jnp.float32).astype(
        jnp.bfloat16
    )
    row_mask = is_valid.reshape(home_rows)
    row_coef = jnp.repeat(weighting, per_device)
    base_rows = frozen_query_rows.reshape(home_rows, -1)
    cotangent = jnp.where(
        row_mask[:, None],
        row_coef[:, None] * output_gradient.reshape(home_rows, -1).astype(jnp.float32),
        0.0,
    ).astype(jnp.bfloat16)
    query_vectors = (
        base_rows.astype(jnp.float32)
        + jnp.dot(lowrank_hidden, up_full, preferred_element_type=jnp.float32)
    ).astype(jnp.bfloat16)
    query_gradient = attend(query_vectors, cotangent, key_rows, value_rows)
    up_term = jnp.dot(lowrank_hidden.T, query_gradient, preferred_element_type=jnp.float32)
    gradient_lowrank = jnp.dot(
        query_gradient, up_full.T, preferred_element_type=jnp.float32
    ).astype(jnp.bfloat16)
    down_term = jnp.dot(normed_input.T, gradient_lowrank, preferred_element_type=jnp.float32)
    down_sum, up_sum = lax.psum((down_term, up_term), ("dp", "fsdp"))
    down_factor_part = adapter_down_factor.shape[0]
    up_factor_part = adapter_up_factor.shape[1]
    grad_down = lax.dynamic_slice_in_dim(
        down_sum, fsdp_index * down_factor_part, down_factor_part, 0
    )
    grad_up = lax.dynamic_slice_in_dim(up_sum, fsdp_index * up_factor_part, up_factor_part, 1)
    return (grad_down, grad_up, seq_ratio)


def solution(mesh):
    in_specs = (
        P(None, "dp", "fsdp", None),
        P(None, "dp", "fsdp", None),
        P(None, "dp", "fsdp", None),
        P(None, "dp", "fsdp"),
        P(),
        P(),
        P("fsdp", None),
        P("fsdp", None),
        P("fsdp", None),
        P(None, "fsdp"),
        P("fsdp"),
    )
    out_specs = (P("fsdp", None), P(None, "fsdp"), P())
    return jax.shard_map(body, mesh=mesh, in_specs=in_specs, out_specs=out_specs, check_vma=False)
```

profile of v0, /device:TPU:17, one launch (start us, length us, event | category | flops | bytes accessed | tf_op | source)
XLA Modules:
  0.0 574.0 jit_solution(2248930495816452318)
XLA Ops:
  7.2 0.7 all-gather.4.cloned.1.call-update
  7.9 0.0 all-gather.6.cloned.1.call-start
  8.0 0.7 all-gather.6.cloned.1.call-update
  8.7 0.0 all-reduce.3.cloned.1.call-start
  8.7 0.9 select_reduce_fusion
  9.6 105.0 %psum.21 = f32[4]{0:T(128)S(1)} all-reduce(f32[4]{0:T(128)S(1)} %get-tuple-element.5), channel_id=1, replica_groups=mesh['dp'=32,'fsdp'=16] {'dp','fsdp'}, use_global_device_ids=true, to_apply=%region_4.5 | all-reduce | flops 4 | bytes 32 | tf_op jit(solution)/shard_map/psum | solution.py:79
  114.6 0.1 lt.29
  114.6 0.7 reshape.122
  115.3 0.7 subtract_multiply_fusion
  116.0 0.1 broadcast_in_dim.20
  116.0 0.1 mul.107
  116.1 2.1 multiply_reduce_fusion
  118.2 0.1 rsqrt.12
  118.3 24.8 %all-gather = bf16[16,1,256]{2,1,0:T(2,128)(2,1)S(1)} all-gather(bf16[1,1,256]{2,1,0:T(2,128)(2,1)S(1)} %reshape.122), channel_id=1, replica_groups=mesh['dp'=32,'fsdp'=16] {'fsdp'}, dimensions={0}, use_global_device_ids=true | all-gather | bytes 8704 | tf_op jit(solution)/shard_map/all_gather | solution.py:84
  143.1 2.2 fusion.1
  145.4 0.3 fusion.12
  145.7 1.3 slice_bitcast_fusion.35
  147.0 1.7 reshape.117
  148.7 1.7 reshape.114
  150.5 1.7 reshape.111
  152.2 0.8 reshape.108
  152.9 24.4 %all_gather.17 = bf16[64,2048]{1,0:T(8,128)(2,1)S(1)} all-gather(bf16[64,128]{1,0:T(8,128)(2,1)S(1)} %copy-done.17), channel_id=1, replica_groups=mesh['dp'=32,'fsdp'=16] {'fsdp'}, dimensions={1}, use_global_device_ids=true | all-gather | bytes 278528 | tf_op jit(solution)/shard_map/all_gather | solution.py:83
  177.3 27.5 %all_gather.16 = bf16[4096,64]{0,1:T(8,128)(2,1)S(1)} all-gather(bf16[256,64]{0,1:T(8,128)(2,1)S(1)} %copy-done.16), channel_id=1, replica_groups=mesh['dp'=32,'fsdp'=16] {'fsdp'}, dimensions={0}, use_global_device_ids=true | all-gather | bytes 557056 | tf_op jit(solution)/shard_map/all_gather | solution.py:82
  204.8 0.8 convolution_convert_fusion.1
  205.6 0.5 fusion.10
  206.0 0.1 copy-done.14
  206.2 0.9 slice_bitcast_fusion.11
  207.1 1.7 multiply_reduce_fusion.4
  208.8 2.0 copy-done
  210.8 0.9 fusion.2
  211.7 0.1 copy.27
  211.9 3.0 fusion.39
  215.0 0.8 fusion.26
  215.7 0.7 copy.28
  216.4 1.9 multiply_reduce_fusion.1
  218.3 1.9 copy-done.1
  220.3 0.9 fusion.8
  221.2 0.8 copy.39
  222.0 3.1 fusion.30
  225.1 0.8 fusion.29
  225.9 0.7 copy.40
  226.6 1.8 multiply_reduce_fusion.2
  228.4 2.0 copy-done.2
  230.3 0.9 fusion.6
  231.3 0.8 copy.35
  232.1 3.1 fusion.33
  235.2 0.8 fusion.28
  235.9 0.7 copy.36
  236.6 1.8 multiply_reduce_fusion.3
  238.4 1.9 copy-done.3
  240.4 1.1 fusion.4
  241.5 0.8 copy.31
  242.3 3.1 fusion.36
  245.4 0.8 fusion.27
  246.2 0.7 copy.32
  246.9 4.8 fusion.21
  251.7 4.8 fusion.24
  256.5 4.8 fusion.23
  261.3 4.8 fusion.22
  266.2 3.6 fusion.25
  269.8 2.2 fusion.70
  272.0 292.6 %all-reduce.3.cloned.1.call-done = (f32[4096,64]{0,1:T(8,128)}, f32[64,2048]{1,0:T(8,128)}) async-done(((f32[4096,64]{0,1:T(8,128)}, f32[64,2048]{1,0:T(8,128)}), (f32[4096,64]{0,1:T(8,128)}, f32[64,2048]{1,0:T(8,128)})) %all-reduce.3.cloned.1.call-update) | async-done | bytes 1572880 | tf_op jit(solution)/shard_map/psum | solution.py:114
  564.6 1.5 constant_dynamic-slice_fusion.1
  566.1 1.4 constant_dynamic-slice_fusion
  (66 shorter events, 0.2 us)
Async XLA Ops:
  7.2 138.2 %copy-start.6 = (bf16[4,64,1,2048]{3,1,2,0:T(8,128)(2,1)S(1)}, bf16[4,64,1,2048]{3,1,2,0:T(8,128)(2,1)}, u32[]{:S(2)}) copy-start(bf16[4,64,1,2048]{3,1,2,0:T(8,128)(2,1)} %param.13) | copy-start | bytes 3145732
  7.2 199.9 %all-gather.4.cloned.1.call-start = ((), (), s32[]{:S(2)}) async-start(), calls=%async_computation | async-start | bytes 1114112 | tf_op jit(solution)/shard_map/all_gather | solution.py:87
  7.9 204.0 %all-gather.6.cloned.1.call-start = ((), (), s32[]{:S(2)}) async-start(), calls=%async_computation.1 | async-start | bytes 1114112 | tf_op jit(solution)/shard_map/all_gather | solution.py:88
  8.7 555.9 %all-reduce.3.cloned.1.call-start = ((), (), s32[]{:S(2)}) async-start(), calls=%async_computation.2 | async-start | bytes 3145728 | tf_op jit(solution)/shard_map/psum | solution.py:114
  114.6 3.7 copy-start.31
  145.3 7.6 %copy-start.17 = (bf16[64,128]{1,0:T(8,128)(2,1)S(1)}, bf16[64,128]{1,0:T(8,128)(2,1)}, u32[]{:S(2)}) copy-start(bf16[64,128]{1,0:T(8,128)(2,1)} %param.20) | copy-start | bytes 49156
  145.4 32.0 %copy-start.16 = (bf16[256,64]{0,1:T(8,128)(2,1)S(1)}, bf16[256,64]{0,1:T(8,128)(2,1)}, u32[]{:S(2)}) copy-start(bf16[256,64]{0,1:T(8,128)(2,1)} %param.19) | copy-start | bytes 98308
  145.7 59.9 %copy-start.5 = (bf16[4,64,1,2048]{3,1,2,0:T(8,128)(2,1)S(1)}, bf16[4,64,1,2048]{3,1,2,0:T(8,128)(2,1)}, u32[]{:S(2)}) copy-start(bf16[4,64,1,2048]{3,1,2,0:T(8,128)(2,1)} %param.12) | copy-start | bytes 3145732
  205.6 0.6 copy-start.14
  208.8 2.0 copy-start
  210.8 4.2 copy-start.10
  211.7 6.6 %copy-start.18 = (f32[256,4]{0,1:T(4,128)}, f32[256,4]{0,1:T(4,128)S(1)}, u32[]{:S(2)}) copy-start(f32[256,4]{0,1:T(4,128)S(1)} %fusion.2) | copy-start | bytes 12292
  216.4 5.6 copy-start.4
  218.3 1.9 copy-start.1
  221.2 0.8 copy-start.19
  222.0 3.1 copy-start.9
  222.0 3.1 copy-start.11
  228.4 2.0 copy-start.2
  231.3 0.8 copy-start.21
  232.1 3.1 copy-start.8
  232.1 3.1 copy-start.12
  238.4 1.9 copy-start.3
  241.5 0.8 copy-start.23
  242.3 3.1 copy-start.7
  242.3 3.1 copy-start.13
  246.9 4.8 copy-start.20
  246.9 4.8 copy-start.25
  251.7 4.8 copy-start.22
  251.7 4.8 copy-start.26
  256.5 4.8 copy-start.24
  256.5 4.8 copy-start.27
  266.2 3.7 copy-start.15
  266.2 3.7 copy-start.28
  266.2 3.7 copy-start.29
  266.2 3.7 copy-start.30
Sparse Core Ops, SparseCore 0:
  10.1 66.9 all-gather.3
  79.2 69.6 all-gather.5
  272.2 292.3 all-reduce.2
where the time goes:
time: 575 us; the launch traced here: 574 us
  waiting for transfers between devices  294 us (51%)
  blocking collectives  182 us (32%)
  matrix products  45.8 us (8%)
  local copies, waits for them, and re-layouts  25.3 us (4%)
  between operations  14.1 us (2%)
  other arithmetic  13.1 us (2%)
    psum x1, waiting for transfers between devices, body(): down_sum, up_sum = lax.psum((down_term, up_term), ('dp', 'fsdp'))  293 us
    psum x1, blocking collectives, body(): seq_ratio = lax.psum(partial_value, ('dp', 'fsdp'))  105 us
    all_gather x1, blocking collectives, body(): lax.all_gather(adapter_down_factor, 'fsdp', axis=0, tiled=True)  27.5 us
    all_gather x1, blocking collectives, body(): lax.all_gather(attention_norm_gain, 'fsdp', axis=0, tiled=True)  24.8 us
    all_gather x1, blocking collectives, body(): lax.all_gather(adapter_up_factor, 'fsdp', axis=1, tiled=True)  24.4 us
    dot_general x4, matrix products, attend(): jnp.einsum('nhj,jd->nhd', grad_score, head_key, preferred_element_type=jn...  19.2 us
    dot_general x4, matrix products, attend(): jnp.einsum('nhj,jd->nhd', weights, head_value, preferred_element_type=jnp...  12.3 us
  transfers between devices with their start and end apart: 3, of which 1 were waited for; matrix products, arithmetic and copies ran while one was open for 3% of the time, Pallas kernels for 0%

commit v1 on v0

--- a/solution.py
+++ b/solution.py
@@ -9,6 +9,12 @@
 KEY_VALUE_HEADS = 4
 target_scale = 1.0
 norm_epsilon = 1e-05
+
+
+def summed_here(x, mesh_axis):
+    parts = lax.all_gather(x, mesh_axis, axis=0, tiled=False)
+    total = parts.sum(axis=0)
+    return total
 
 
 def attend(query_vectors, cotangent, key_rows, value_rows):
@@ -76,7 +82,7 @@
     position = (dp_index * per_device + local_rows) * fsdp_count + fsdp_index
     is_valid = position[None, :] < lengths[:, None]
     partial_value = jnp.sum(jnp.where(is_valid, token_log_ratio[:, :, 0], 0.0), axis=1)
-    seq_ratio = lax.psum(partial_value, ("dp", "fsdp"))
+    seq_ratio = summed_here(partial_value, ("dp", "fsdp"))
     weighting = 2.0 * (seq_ratio - target_scale * (response_win_probability - 0.5)) / responses
     down_full, up_full, gain_full = (
         lax.all_gather(adapter_down_factor, "fsdp", axis=0, tiled=True),

time: 575 us -> 551 us (0.958)
  blocking collectives: 182 us -> 203 us
  waiting for transfers between devices: 294 us -> 274 us
  local copies, waits for them, and re-layouts: 25.3 us -> 10 us
  other arithmetic: 13.1 us -> 7.15 us
    unnamed x0 -> x1, blocking collectives: none -> 116 us
    psum x1 -> x0, blocking collectives: 105 us -> none  [body(): seq_ratio = lax.psum(partial_value, ('dp', 'fsdp'))]
    psum x1, waiting for transfers between devices: 293 us -> 273 us  [body(): down_sum, up_sum = lax.psum((down_term, up_term), ('dp', 'fsdp'))]
    all_gather x1, blocking collectives: 24.8 us -> 32.6 us  [body(): lax.all_gather(attention_norm_gain, 'fsdp', axis=0, tiled=True)]
    reshape x4 -> x0, local copies, waits for them, and re-layouts: 5.92 us -> none  [attend(): cotangent[:, head_start:head_stop]]
where the time goes in v1:
time: 551 us
  waiting for transfers between devices  274 us (50%)
  blocking collectives  203 us (37%)
  matrix products  42.5 us (8%)
  between operations  14 us (3%)
  local copies, waits for them, and re-layouts  10 us (2%)
  other arithmetic  7.15 us (1%)
    psum x1, waiting for transfers between devices, body(): down_sum, up_sum = lax.psum((down_term, up_term), ('dp', 'fsdp'))  273 us
    unnamed x1, blocking collectives  116 us
    all_gather x1, blocking collectives, body(): lax.all_gather(attention_norm_gain, 'fsdp', axis=0, tiled=True)  32.6 us
    all_gather x1, blocking collectives, body(): lax.all_gather(adapter_down_factor, 'fsdp', axis=0, tiled=True)  27.4 us
    all_gather x1, blocking collectives, body(): lax.all_gather(adapter_up_factor, 'fsdp', axis=1, tiled=True)  26.9 us
    dot_general x4, matrix products, attend(): jnp.einsum('nhj,jd->nhd', grad_score, head_key, preferred_element_type=jn...  19.1 us
    dot_general x4, matrix products, attend(): jnp.einsum('nhj,jd->nhd', weights, head_value, preferred_element_type=jnp...  12.8 us
  transfers between devices with their start and end apart: 3, of which 1 were waited for; matrix products, arithmetic and copies ran while one was open for 3% of the time, Pallas kernels for 0%

profile of v1, /device:TPU:17, one launch (start us, length us, event | category | flops | bytes accessed | tf_op | source)
XLA Modules:
  0.0 550.9 jit_solution(14064353366586891318)
XLA Ops:
  7.2 0.0 copy-start.4
  7.2 0.0 all-gather.5.cloned.1.call-start
  7.2 0.7 all-gather.5.cloned.1.call-update
  7.9 0.0 all-gather.7.cloned.1.call-start
  8.0 0.7 all-gather.7.cloned.1.call-update
  8.7 0.0 all-reduce.4.cloned.1.call-start
  8.7 0.7 reshape.125
  9.4 32.6 %all-gather.1 = bf16[16,1,256]{2,1,0:T(2,128)(2,1)S(1)} all-gather(bf16[1,1,256]{2,1,0:T(2,128)(2,1)S(1)} %reshape.125), channel_id=1, replica_groups=mesh['dp'=32,'fsdp'=16] {'fsdp'}, dimensions={0}, use_global_device_ids=true | all-gather | bytes 8704 | tf_op jit(solution)/shard_map/all_gather | solution.py:90
  42.0 2.1 multiply_reduce_fusion
  44.1 0.1 rsqrt.12
  44.2 27.4 %all_gather.22 = bf16[4096,64]{0,1:T(8,128)(2,1)S(1)} all-gather(bf16[256,64]{0,1:T(8,128)(2,1)} %param.19), channel_id=1, replica_groups=mesh['dp'=32,'fsdp'=16] {'fsdp'}, dimensions={0}, use_global_device_ids=true | all-gather | bytes 557056 | tf_op jit(solution)/shard_map/all_gather | solution.py:88
  71.6 26.9 %all_gather.23 = bf16[64,2048]{1,0:T(8,128)(2,1)S(1)} all-gather(bf16[64,128]{1,0:T(8,128)(2,1)} %param.20), channel_id=1, replica_groups=mesh['dp'=32,'fsdp'=16] {'fsdp'}, dimensions={1}, use_global_device_ids=true | all-gather | bytes 278528 | tf_op jit(solution)/shard_map/all_gather | solution.py:89
  98.5 0.0 copy-done.4
  98.5 0.7 fusion.1
  99.2 0.0 copy-start.5
  99.2 1.3 copy-done.5
  100.6 0.8 convolution_convert_fusion.1
  101.4 0.5 fusion.10
  101.8 0.1 slice_bitcast_fusion.11
  102.0 0.2 select_reduce_fusion
  102.1 0.3 dynamic-update-slice
  102.4 116.1 %all-reduce = f32[2048]{0:T(1024)S(1)} all-reduce(f32[2048]{0:T(1024)S(1)} %dynamic-update-slice), channel_id=2, replica_groups=mesh['dp'=32,'fsdp'=16] {'dp','fsdp'}, use_global_device_ids=true, to_apply=%add | all-reduce | flops 2048 | bytes 16384
  218.5 0.3 reshape.122
  218.8 0.1 reduce_sum.102
  218.9 0.0 copy-done.13
  218.9 0.0 copy-start.11
  218.9 0.1 broadcast_in_dim.20
  219.0 0.1 mul.107
  219.1 0.1 lt.29
  219.2 0.3 fusion.12
  219.5 0.1 fusion.66
  219.6 0.1 copy.89
  219.7 0.1 copy.96
  219.8 0.1 copy.103
  220.0 0.1 copy.110
  220.1 0.0 all-gather.5.cloned.1.call-done
  220.2 1.8 multiply_reduce_fusion.4
  222.0 0.0 copy-done.11
  222.0 0.8 multiply_reduce_fusion.3
  222.8 0.9 fusion.2
  223.7 0.2 copy-done.3
  223.9 0.9 fusion.4
  224.9 0.4 copy-done.1
  225.3 0.8 multiply_reduce_fusion.2
  226.1 0.9 fusion.6
  227.0 1.0 copy-done.2
  228.0 0.8 multiply_reduce_fusion.1
  228.8 1.9 copy-done
  230.8 0.9 fusion.8
  231.7 0.0 all-gather.7.cloned.1.call-done
  231.7 3.2 fusion.29
  234.9 4.8 fusion.25
  239.7 3.2 fusion.30
  243.0 4.4 fusion.26
  247.3 3.2 fusion.31
  250.5 4.8 fusion.27
  255.4 3.2 fusion.32
  258.6 5.0 fusion.28
  263.6 2.3 fusion.54
  265.9 3.0 fusion.33
  268.9 0.0 all-reduce.4.cloned.1.call-update
  268.9 272.6 %all-reduce.4.cloned.1.call-done = (f32[4096,64]{0,1:T(8,128)}, f32[64,2048]{1,0:T(8,128)}) async-done(((f32[4096,64]{0,1:T(8,128)}, f32[64,2048]{1,0:T(8,128)}), (f32[4096,64]{0,1:T(8,128)}, f32[64,2048]{1,0:T(8,128)})) %all-reduce.4.cloned.1.call-update) | async-done | bytes 1572880 | tf_op jit(solution)/shard_map/psum | solution.py:120
  541.5 1.5 constant_dynamic-slice_fusion.1
  543.0 1.4 constant_dynamic-slice_fusion
  (24 shorter events, 0.1 us)
Async XLA Ops:
  7.2 91.3 %copy-start.4 = (bf16[4,64,1,4096]{3,1,2,0:T(8,128)(2,1)S(1)}, bf16[4,64,1,4096]{3,1,2,0:T(8,128)(2,1)}, u32[]{:S(2)}) copy-start(bf16[4,64,1,4096]{3,1,2,0:T(8,128)(2,1)} %param.11) | copy-start | bytes 6291460
  7.2 213.0 %all-gather.5.cloned.1.call-start = ((), (), s32[]{:S(2)}) async-start(), calls=%async_computation | async-start | bytes 1114112 | tf_op jit(solution)/shard_map/all_gather | solution.py:93
  7.9 223.8 %all-gather.7.cloned.1.call-start = ((), (), s32[]{:S(2)}) async-start(), calls=%async_computation.1 | async-start | bytes 1114112 | tf_op jit(solution)/shard_map/all_gather | solution.py:94
  8.7 532.8 %all-reduce.4.cloned.1.call-start = ((), (), s32[]{:S(2)}) async-start(), calls=%async_computation.2 | async-start | bytes 3145728 | tf_op jit(solution)/shard_map/psum | solution.py:120
  44.1 57.2 %copy-start.7 = (bf16[4,64,1,2048]{3,1,2,0:T(8,128)(2,1)S(1)}, bf16[4,64,1,2048]{3,1,2,0:T(8,128)(2,1)}, u32[]{:S(2)}) copy-start(bf16[4,64,1,2048]{3,1,2,0:T(8,128)(2,1)} %param.12) | copy-start | bytes 3145732
  99.2 1.4 copy-start.5
  100.6 1.4 copy-start.10
  100.6 1.4 copy-start.12
  100.6 118.3 %copy-start.13 = (f32[4]{0:T(128)S(1)}, f32[4]{0:T(128)}, u32[]{:S(2)}) copy-start(f32[4]{0:T(128)} %param.16) | copy-start | bytes 52
  100.6 118.6 %copy-start.8 = (bf16[4,64,1,2048]{3,1,2,0:T(8,128)(2,1)S(1)}, bf16[4,64,1,2048]{3,1,2,0:T(8,128)(2,1)}, u32[]{:S(2)}) copy-start(bf16[4,64,1,2048]{3,1,2,0:T(8,128)(2,1)} %param.13) | copy-start | bytes 3145732
  218.9 3.1 copy-start.11
  220.1 1.9 copy-start.9
  222.0 2.0 copy-start.3
  222.8 2.5 copy-start.1
  226.1 2.0 copy-start.2
  228.8 1.9 copy-start
  258.6 5.0 copy-start.14
  258.6 7.3 %copy-start.6 = (bf16[256,4096]{1,0:T(8,128)(2,1)S(1)}, bf16[256,4096]{1,0:T(8,128)(2,1)}, u32[]{:S(2)}) copy-start(bf16[256,4096]{1,0:T(8,128)(2,1)} %copy-done.5) | copy-start | bytes 6291460
Sparse Core Ops, SparseCore 0:
  10.1 67.6 all-gather.4
  79.9 69.0 all-gather.6
  269.0 272.4 all-reduce.3
